TPU v7x, 32 devices: a whole 2x2x4 slice. The times are simulated.
32 devices in a mesh: groups: 2 (over y), ctx: 16 (over z, x, core).
Axes of the slice: x: 2, y: 2, z: 4, core: 2. Of those that a mesh axis runs over, the one named last changes fastest.
Arguments:
- outer_gate: bfloat16 [32768, 256], P(('groups', 'ctx')), parts along dimension 0, may hold values from -6 to 6
- inner_gate: bfloat16 [32768, 256], P(('groups', 'ctx')), parts along dimension 0, may hold values from -6 to 6
- values: bfloat16 [32768, 256], P(('groups', 'ctx')), parts along dimension 0, may hold values from -6 to 6
- cotangent: bfloat16 [32768, 256], P(('groups', 'ctx')), parts along dimension 0, may hold values from -6 to 6
- residue: float32 [256, 16], replicated, may hold values from -0.5 to 0.5
- decay_rate: float32 [256, 16], replicated, may hold values from 1.8310547e-05 to 0.1
- skip_gain: float32 [256], replicated, may hold values from -4 to 4
Outputs:
- layer_out: bfloat16 [32768, 256], P(('groups', 'ctx')), parts along dimension 0
- grad_outer: bfloat16 [32768, 256], P(('groups', 'ctx')), parts along dimension 0
- grad_inner: bfloat16 [32768, 256], P(('groups', 'ctx')), parts along dimension 0
- grad_values: bfloat16 [32768, 256], P(('groups', 'ctx')), parts along dimension 0
There are 2 independent parts, one for each index of `groups`. A program takes and returns all parts, laid end to end along the dimension named above; an argument that names none is the same for every part. Nothing has to cross between parts.
All inputs are finite; a program needn't handle non-finite values.
Results may differ from a plain program's by a relative error of at most 0.005.
Values sent between devices are 32-bit elements; how exact they have to be, the bound alone decides.
No kernel may reach another device: no remote copies, remote signals or barrier semaphores. Data moves between devices by JAX's collectives and lax.ppermute only.
A program may use at most 128 MiB of HBM per device.

v0:
```python
import jax
import jax.numpy as jnp
from jax import lax
from jax.sharding import PartitionSpec as P


def product(pattern, first, second):
    return jnp.einsum(pattern, first, second, precision=lax.Precision.HIGH)


def shards(outer_gate, inner_gate, values, cotangent, residue, decay_rate, skip_gain):
    row_count, channels = values.shape
    block_width = min(64, row_count)
    block_count = row_count // block_width
    position = lax.axis_index("ctx")
    rate_table = decay_rate.T
    pole_weight = residue.T
    mixed_input = (inner_gate.astype(jnp.float32) * values.astype(jnp.float32)).astype(jnp.bfloat16)
    mixed_float = lax.optimization_barrier(mixed_input).astype(jnp.float32)
    offsets = jnp.arange(block_width, dtype=jnp.float32)
    enter_table = jnp.exp(-rate_table[None] * (offsets + 1.0)[:, None, None])
    leave_table = jnp.exp(-rate_table[None] * (block_width - 1.0 - offsets)[:, None, None])
    sections = jnp.arange(block_count, dtype=jnp.float32)
    powers = jnp.exp(-rate_table[None] * (block_width * sections)[:, None, None])
    reverse_powers = powers[::-1]
    later_index = jnp.arange(block_count)[:, None]
    earlier_index = jnp.arange(block_count)[None, :]
    spacing = jnp.maximum(later_index - earlier_index - 1, 0).astype(jnp.float32)
    decayed = jnp.exp(-rate_table[None, None] * (block_width * spacing)[:, :, None, None])
    carry_table = jnp.where((earlier_index < later_index)[:, :, None, None], decayed, 0.0)
    tap_values = jnp.sum(
        pole_weight[None] * jnp.exp(-rate_table[None] * offsets[:, None, None]), axis=1
    )
    differ = jnp.arange(block_width)[:, None] - jnp.arange(block_width)[None, :]
    lag_onehot = (differ[:, :, None] == jnp.arange(block_width)[None, None, :]).astype(jnp.float32)
    kernel = jnp.einsum("tsl,lc->tsc", lag_onehot, tap_values, precision=lax.Precision.HIGHEST)
    pieces = mixed_float.reshape(block_count, block_width, channels)
    span_states = product("nsc,skc->nkc", pieces, leave_table)
    own_state = jnp.sum(span_states * reverse_powers, axis=0)
    within = product("nsc,tsc->ntc", pieces, kernel)
    carried = product("mjkc,jkc->mkc", carry_table, span_states)
    across = product("mkc,tkc->mtc", carried * pole_weight[None], enter_table)
    piece = lax.all_gather(own_state[None], "ctx", axis=0, tiled=True)
    anchor = jnp.arange(piece.shape[0])
    distance = position - anchor - 1
    scaled = jnp.exp(
        -rate_table[None]
        * (row_count * jnp.maximum(distance, 0)).astype(jnp.float32)[:, None, None]
    )
    weight_rows = jnp.where((distance >= 0)[:, None, None], scaled, 0.0)
    gathered = jnp.sum(weight_rows * piece, axis=0)
    remote = product("mkc,tkc->mtc", powers * (pole_weight * gathered)[None], enter_table)
    response = skip_gain[None, :] * mixed_float + (within + across + remote).reshape(
        row_count, channels
    )
    layer_out = (outer_gate.astype(jnp.float32) * response).astype(jnp.bfloat16)
    grad_outer = (cotangent.astype(jnp.float32) * response).astype(jnp.bfloat16)
    grad_response = outer_gate.astype(jnp.float32) * cotangent.astype(jnp.float32)
    grad_pieces = grad_response.reshape(block_count, block_width, channels)
    span_adjoint = product("ntc,tkc->nkc", grad_pieces, enter_table)
    own_adjoint = jnp.sum(span_adjoint * powers, axis=0)
    within_back = product("ntc,tsc->nsc", grad_pieces, kernel)
    carried_back = product("mjkc,mkc->jkc", carry_table, span_adjoint)
    across_back = product("jkc,skc->jsc", carried_back * pole_weight[None], leave_table)
    piece = lax.all_gather(own_adjoint[None], "ctx", axis=0, tiled=True)
    anchor = jnp.arange(piece.shape[0])
    distance = anchor - position - 1
    scaled = jnp.exp(
        -rate_table[None]
        * (row_count * jnp.maximum(distance, 0)).astype(jnp.float32)[:, None, None]
    )
    weight_rows = jnp.where((distance >= 0)[:, None, None], scaled, 0.0)
    suffix = jnp.sum(weight_rows * piece, axis=0)
    decoded = product("nkc,skc->nsc", reverse_powers * (pole_weight * suffix)[None], leave_table)
    grad_mixed = skip_gain[None, :] * grad_response + (within_back + across_back + decoded).reshape(
        row_count, channels
    )
    grad_inner = (grad_mixed * values.astype(jnp.float32)).astype(jnp.bfloat16)
    grad_values = (grad_mixed * inner_gate.astype(jnp.float32)).astype(jnp.bfloat16)
    return (layer_out, grad_outer, grad_inner, grad_values)


def solution(mesh):
    return jax.shard_map(
        shards,
        mesh=mesh,
        in_specs=(
            P(("groups", "ctx"), None),
            P(("groups", "ctx"), None),
            P(("groups", "ctx"), None),
            P(("groups", "ctx"), None),
            P(),
            P(),
            P(),
        ),
        out_specs=(
            P(("groups", "ctx"), None),
            P(("groups", "ctx"), None),
            P(("groups", "ctx"), None),
            P(("groups", "ctx"), None),
        ),
        check_vma=False,
    )
```

profile of v0, /device:TPU:0, one launch (start us, length us, event | category | flops | bytes accessed | tf_op | source)
XLA Modules:
  0.0 141.4 jit_solution(13211322422101003060)
XLA Ops:
  3.6 0.7 negate_bitcast_fusion
  5.0 0.8 copy.57
  5.9 2.3 %multiply_reduce_fusion.4 = f32[64,256]{0,1:T(8,128)} fusion(f32[16,256]{0,1:T(8,128)S(1)} %copy.58, f32[16,256]{0,1:T(8,128)S(1)} %bitcast.60), kind=kLoop, calls=%fused_computation.26 | loop fusion | flops 770048 | bytes 98304 | tf_op jit(solution)/shard_map/reduce_sum | solution.py:31
  8.1 1.3 fusion.17
  9.5 1.0 copy.61
  10.5 1.1 convert_multiply_fusion
  11.6 2.5 %copy.68 = f32[16,64,256]{1,0,2:T(8,128)S(1)} copy(f32[16,64,256]{2,1,0:T(8,128)} %bitcast.59) | data formatting | bytes 2097152 | tf_op jit(solution)/shard_map/reshape | solution.py:59
  14.1 4.9 %fusion.14 = f32[64,64,256]{2,1,0:T(8,128)} fusion(s32[64,64]{1,0:T(8,128)S(1)} %iota_subtract_fusion, f32[64,256]{0,1:T(8,128)} %multiply_reduce_fusion.4), kind=kOutput, calls=%fused_computation.28 | convolution fusion | flops 805568512 | bytes 4276224 | tf_op jit(solution)/shard_map/tsl,lc->tsc/dot_general | solution.py:36
  19.0 9.1 %copy.60 = f32[64,64,256]{1,0,2:T(8,128)} copy(f32[64,64,256]{2,1,0:T(8,128)} %fusion.14) | data formatting | bytes 8388608 | tf_op jit(solution)/shard_map/tsl,lc->tsc/dot_general | solution.py:36
  28.2 4.0 %multiply_exponential_fusion = (f32[16,16,256]{1,0,2:T(8,128)}, f32[16,256]{0,1:T(8,128)S(1)}, f32[256,16,16]{1,2,0:T(8,128)}) fusion(f32[16]{0:T(128)S(1)} %iota_multiply_fusion, f32[16,256]{0,1:T(8,128)S(1)} %copy.58, f32[16,64,256]{1,0,2:T(8,128)S(1)} %copy.68, f32[64]{0:T(128)S(1)} %iota_add_fusion), kind=kOutput, calls=%fused_computation.20 | convolution fusion | flops 25620480 | bytes 1605952 | tf_op jit(solution)/shard_map/ntc,tkc->nkc/dot_general | solution.py:8
  32.2 2.4 %rev.3 = f32[16,16,256]{1,0,2:T(8,128)S(1)} reverse(f32[16,16,256]{1,0,2:T(8,128)} %get-tuple-element.12), dimensions={0} | reverse | bytes 524288 | tf_op jit(solution)/shard_map/rev | solution.py:25
  34.7 25.5 %all-gather.1 = f32[256,256]{1,0:T(8,128)} all-gather(f32[16,256]{1,0:T(8,128)S(1)} %copy.70), channel_id=3, replica_groups=mesh['groups'=2,'ctx'=16] {'ctx'}, dimensions={0}, use_global_device_ids=true | all-gather | bytes 278528 | tf_op jit(solution)/shard_map/all_gather | solution.py:65
  60.2 3.2 %copy.92 = f32[16,256,16]{1,0,2:T(8,128)} copy(f32[16,256,16]{0,2,1:T(8,128)} %bitcast.56) | data formatting | bytes 524288
  63.4 2.7 %multiply_reduce_fusion = f32[16,256,16]{1,0,2:T(8,128)} fusion(f32[16,256,16]{1,0,2:T(8,128)} %copy.92, f32[16,16]{1,0:T(8,128)S(1)} %copy-done.11, f32[16,256]{1,0:T(8,128)S(1)} %copy-done.9, pred[16,16]{1,0:T(8,128)(4,1)S(1)} %copy-done.17), kind=kLoop, calls=%fused_computation | loop fusion | flops 4128768 | bytes 541952
  66.1 3.4 %copy.89 = f32[16,256,16]{0,2,1:T(8,128)} copy(f32[16,256,16]{1,0,2:T(8,128)} %multiply_reduce_fusion) | data formatting | bytes 524288 | tf_op jit(solution)/shard_map/mjkc,mkc->jkc/dot_general | solution.py:8
  69.5 4.3 %fusion = f32[256,64,16]{1,2,0:T(8,128)} fusion(f32[16,256,16]{0,2,1:T(8,128)} %copy.89, f32[16,256]{0,1:T(8,128)S(1)} %bitcast.61, f32[64]{0:T(128)S(1)} %copy-done.13, f32[16,256]{0,1:T(8,128)S(1)} %copy.58), kind=kOutput, calls=%fused_computation.3 | convolution fusion | flops 25493504 | bytes 1343744 | tf_op jit(solution)/shard_map/jkc,skc->jsc/dot_general | solution.py:8
  73.7 3.4 %copy.71 = f32[16,16,256]{1,0,2:T(8,128)} copy(f32[16,16,256]{2,1,0:T(8,128)} %bitcast.63) | data formatting | bytes 524288 | tf_op jit(solution)/shard_map/all_gather | solution.py:65
  77.1 3.1 %fusion.5 = (f32[16,256]{0,1:T(8,128)S(1)}, f32[256,16,16]{1,2,0:T(8,128)}) fusion(f32[16,16,256]{1,0,2:T(8,128)S(1)} %rev.3, bf16[16,64,256]{1,0,2:T(8,128)(2,1)S(1)} %copy.61, f32[64]{0:T(128)S(1)} %copy-done.13, f32[16,256]{0,1:T(8,128)S(1)} %copy.58), kind=kOutput, calls=%fused_computation.10 | convolution fusion | flops 25554944 | bytes 1081600 | tf_op jit(solution)/shard_map/nsc,skc->nkc/dot_general | solution.py:8
  80.3 3.2 %copy.91 = f32[16,256,16]{1,0,2:T(8,128)} copy(f32[16,256,16]{0,2,1:T(8,128)} %bitcast.57) | data formatting | bytes 524288
  83.6 2.7 %multiply_reduce_fusion.1 = f32[16,256,16]{1,0,2:T(8,128)} fusion(f32[16,256,16]{1,0,2:T(8,128)} %copy.91, f32[16,16]{1,0:T(8,128)S(1)} %copy-done.12, f32[16,256]{1,0:T(8,128)S(1)} %copy-done.10, pred[16,16]{1,0:T(8,128)(4,1)S(1)} %copy-done.18), kind=kLoop, calls=%fused_computation.1 | loop fusion | flops 4128768 | bytes 541952
  86.3 19.5 %all-gather = f32[256,256]{1,0:T(8,128)} all-gather(f32[16,256]{1,0:T(8,128)S(1)} %copy.64), channel_id=2, replica_groups=mesh['groups'=2,'ctx'=16] {'ctx'}, dimensions={0}, use_global_device_ids=true | all-gather | bytes 278528 | tf_op jit(solution)/shard_map/all_gather | solution.py:43
  105.8 3.4 %copy.65 = f32[16,16,256]{1,0,2:T(8,128)} copy(f32[16,16,256]{2,1,0:T(8,128)} %bitcast.64) | data formatting | bytes 524288 | tf_op jit(solution)/shard_map/all_gather | solution.py:43
  109.2 3.9 %multiply_reduce_fusion.2 = (f32[16,256]{0,1:T(8,128)S(1)}, f32[16,256]{0,1:T(8,128)S(1)}) fusion(f32[16,16,256]{1,0,2:T(8,128)} %copy.71, f32[16]{0:T(128)S(1)} %copy-done.22, f32[16,256]{0,1:T(8,128)S(1)} %copy.58, pred[16]{0:T(512)(128)(4,1)S(1)} %copy-done.25, f32[16,16,256]{1,0,2:T(8,128)} %copy.65, f32[16]{0:T(128)S(1)} %copy-done.23, ...), kind=kLoop, calls=%fused_computation.14 | loop fusion | flops 516096 | bytes 573600 | tf_op jit(solution)/shard_map/reduce_sum | solution.py:73
  113.2 1.4 fusion.6
  115.4 5.8 %add_bitcast_fusion = f32[16,64,256]{1,0,2:T(8,128)S(1)} fusion(f32[256,64,16]{1,2,0:T(8,128)S(1)} %fusion.6, f32[256,64,16]{1,2,0:T(8,128)S(1)} %copy-done.2, f32[64,64,256]{1,0,2:T(8,128)} %copy.60, f32[16,64,256]{1,0,2:T(8,128)S(1)} %copy-done.1), kind=kOutput, calls=%fused_computation.11 | convolution fusion | flops 101187584 | bytes 8388608 | tf_op jit(solution)/shard_map/ntc,tsc->nsc/dot_general | solution.py:8
  121.2 2.1 %copy.72 = f32[16,64,256]{2,1,0:T(8,128)} copy(f32[16,64,256]{1,0,2:T(8,128)S(1)} %add_bitcast_fusion) | data formatting | bytes 2097152 | tf_op jit(solution)/shard_map/add | solution.py:75
  123.3 2.2 %copy.81 = f32[16,256,16]{0,2,1:T(8,128)S(1)} copy(f32[16,256,16]{1,0,2:T(8,128)} %multiply_reduce_fusion.1) | data formatting | bytes 524288 | tf_op jit(solution)/shard_map/mjkc,jkc->mkc/dot_general | solution.py:8
  125.5 1.4 fusion.3
  127.0 1.6 %fusion.9 = f32[256,64,16]{1,2,0:T(8,128)S(1)} fusion(f32[16,256]{0,1:T(8,128)S(1)} %get-tuple-element.15, f32[16]{0:T(128)S(1)} %copy-done.21, f32[16,256]{0,1:T(8,128)S(1)} %copy.58, f32[64]{0:T(128)S(1)} %copy-done.16), kind=kOutput, calls=%fused_computation.17 | convolution fusion | flops 25559040 | bytes 1081664 | tf_op jit(solution)/shard_map/mkc,tkc->mtc/dot_general | solution.py:8
  128.6 6.9 %add_bitcast_fusion.1 = f32[16,64,256]{1,0,2:T(8,128)S(1)} fusion(f32[256,64,16]{1,2,0:T(8,128)S(1)} %fusion.9, f32[256,64,16]{1,2,0:T(8,128)S(1)} %fusion.3, f32[64,64,256]{1,0,2:T(8,128)} %copy.60, bf16[16,64,256]{1,0,2:T(8,128)(2,1)S(1)} %copy.61), kind=kOutput, calls=%fused_computation.16 | convolution fusion | flops 101187584 | bytes 7864320 | tf_op jit(solution)/shard_map/nsc,tsc->ntc/dot_general | solution.py:8
  135.6 2.0 %copy.66 = f32[16,64,256]{2,1,0:T(8,128)} copy(f32[16,64,256]{1,0,2:T(8,128)S(1)} %add_bitcast_fusion.1) | data formatting | bytes 2097152 | tf_op jit(solution)/shard_map/add | solution.py:53
  137.6 3.8 %fusion.19 = (bf16[1024,256]{1,0:T(8,128)(2,1)}, bf16[1024,256]{1,0:T(8,128)(2,1)}, bf16[1024,256]{1,0:T(8,128)(2,1)}, bf16[1024,256]{1,0:T(8,128)(2,1)}) fusion(bf16[1024,256]{1,0:T(8,128)(2,1)} %param.10, f32[16,64,256]{2,1,0:T(8,128)} %copy.66, bf16[1024,256]{1,0:T(8,128)(2,1)S(1)} %copy-done.4, f32[256]{0:T(256)S(1)} %copy-done.19, ...), kind=kLoop, calls=%fused_computation.39 | loop fusion | flops 4718592 | bytes 6816768 | tf_op jit(solution)/shard_map/convert_element_type | solution.py:57
  (64 shorter events, 4.7 us)
Async XLA Ops:
  0.6 9.8 %copy-start.6 = (bf16[1024,256]{1,0:T(8,128)(2,1)S(1)}, bf16[1024,256]{1,0:T(8,128)(2,1)}, u32[]{:S(2)}) copy-start(bf16[1024,256]{1,0:T(8,128)(2,1)} %param.10) | copy-start | bytes 1572868
  0.6 9.8 %copy-start.7 = (bf16[1024,256]{1,0:T(8,128)(2,1)S(1)}, bf16[1024,256]{1,0:T(8,128)(2,1)}, u32[]{:S(2)}) copy-start(bf16[1024,256]{1,0:T(8,128)(2,1)} %param.7) | copy-start | bytes 1572868
  0.7 27.5 %copy-start.15 = (f32[64]{0:T(128)}, f32[64]{0:T(128)S(1)}, u32[]{:S(2)}) copy-start(f32[64]{0:T(128)S(1)} %iota_add_fusion) | copy-start | bytes 772
  1.2 26.9 %copy-start.20 = (f32[16]{0:T(128)}, f32[16]{0:T(128)S(1)}, u32[]{:S(2)}) copy-start(f32[16]{0:T(128)S(1)} %iota_multiply_fusion) | copy-start | bytes 196
  4.3 0.6 copy-start.8
  9.5 2.1 %copy-start.3 = (bf16[1024,256]{1,0:T(8,128)(2,1)}, bf16[1024,256]{1,0:T(8,128)(2,1)S(1)}, u32[]{:S(2)}) copy-start(bf16[1024,256]{1,0:T(8,128)(2,1)S(1)} %fusion.17) | copy-start | bytes 1572868
  14.1 14.1 %copy-start = (f32[16,64,256]{1,0,2:T(8,128)}, f32[16,64,256]{1,0,2:T(8,128)S(1)}, u32[]{:S(2)}) copy-start(f32[16,64,256]{1,0,2:T(8,128)S(1)} %copy.68) | copy-start | bytes 3145732
  34.6 28.7 %copy-start.9 = (f32[16,256]{1,0:T(8,128)S(1)}, f32[16,256]{1,0:T(8,128)}, u32[]{:S(2)}) copy-start(f32[16,256]{1,0:T(8,128)} %copy-done.8) | copy-start | bytes 49156
  34.6 28.7 %copy-start.11 = (f32[16,16]{1,0:T(8,128)S(1)}, f32[16,16]{1,0:T(8,128)}, u32[]{:S(2)}) copy-start(f32[16,16]{1,0:T(8,128)} %convert_multiply_fusion.6) | copy-start | bytes 3076
  34.6 28.7 %copy-start.17 = (pred[16,16]{1,0:T(8,128)(4,1)S(1)}, pred[16,16]{1,0:T(8,128)(4,1)}, u32[]{:S(2)}) copy-start(pred[16,16]{1,0:T(8,128)(4,1)} %iota_compare_fusion.2) | copy-start | bytes 772
  63.4 6.1 %copy-start.13 = (f32[64]{0:T(128)S(1)}, f32[64]{0:T(128)}, u32[]{:S(2)}) copy-start(f32[64]{0:T(128)} %iota_subtract_fusion.1) | copy-start | bytes 772
  80.3 3.2 %copy-start.10 = (f32[16,256]{1,0:T(8,128)S(1)}, f32[16,256]{1,0:T(8,128)}, u32[]{:S(2)}) copy-start(f32[16,256]{1,0:T(8,128)} %copy-done.8) | copy-start | bytes 49156
  80.3 3.2 %copy-start.12 = (f32[16,16]{1,0:T(8,128)S(1)}, f32[16,16]{1,0:T(8,128)}, u32[]{:S(2)}) copy-start(f32[16,16]{1,0:T(8,128)} %convert_multiply_fusion.6) | copy-start | bytes 3076
  80.3 3.2 %copy-start.18 = (pred[16,16]{1,0:T(8,128)(4,1)S(1)}, pred[16,16]{1,0:T(8,128)(4,1)}, u32[]{:S(2)}) copy-start(pred[16,16]{1,0:T(8,128)(4,1)} %iota_compare_fusion.2) | copy-start | bytes 772
  83.5 25.7 %copy-start.22 = (f32[16]{0:T(128)S(1)}, f32[16]{0:T(128)}, u32[]{:S(2)}) copy-start(f32[16]{0:T(128)} %get-tuple-element.19) | copy-start | bytes 196
  83.5 25.7 %copy-start.23 = (f32[16]{0:T(128)S(1)}, f32[16]{0:T(128)}, u32[]{:S(2)}) copy-start(f32[16]{0:T(128)} %get-tuple-element.20) | copy-start | bytes 196
  83.5 25.7 %copy-start.24 = (pred[16]{0:T(512)(128)(4,1)S(1)}, pred[16]{0:T(512)(128)(4,1)}, u32[]{:S(2)}) copy-start(pred[16]{0:T(512)(128)(4,1)} %get-tuple-element.21) | copy-start | bytes 52
  83.6 25.7 %copy-start.25 = (pred[16]{0:T(512)(128)(4,1)S(1)}, pred[16]{0:T(512)(128)(4,1)}, u32[]{:S(2)}) copy-start(pred[16]{0:T(512)(128)(4,1)} %get-tuple-element.22) | copy-start | bytes 52
  109.2 3.9 %copy-start.14 = (f32[64]{0:T(128)S(1)}, f32[64]{0:T(128)}, u32[]{:S(2)}) copy-start(f32[64]{0:T(128)} %iota_subtract_fusion.1) | copy-start | bytes 772
  113.2 1.6 %copy-start.1 = (f32[16,64,256]{1,0,2:T(8,128)S(1)}, f32[16,64,256]{1,0,2:T(8,128)}, u32[]{:S(2)}) copy-start(f32[16,64,256]{1,0,2:T(8,128)} %copy-done) | copy-start | bytes 3145732
  113.2 2.2 %copy-start.2 = (f32[256,64,16]{1,2,0:T(8,128)S(1)}, f32[256,64,16]{1,2,0:T(8,128)}, u32[]{:S(2)}) copy-start(f32[256,64,16]{1,2,0:T(8,128)} %fusion) | copy-start | bytes 3145732
  121.2 4.3 %copy-start.16 = (f32[64]{0:T(128)S(1)}, f32[64]{0:T(128)}, u32[]{:S(2)}) copy-start(f32[64]{0:T(128)} %copy-done.15) | copy-start | bytes 772
  125.5 1.4 copy-start.21
  135.5 2.0 %copy-start.4 = (bf16[1024,256]{1,0:T(8,128)(2,1)S(1)}, bf16[1024,256]{1,0:T(8,128)(2,1)}, u32[]{:S(2)}) copy-start(bf16[1024,256]{1,0:T(8,128)(2,1)} %copy-done.3) | copy-start | bytes 1572868
  135.5 2.0 %copy-start.5 = (bf16[1024,256]{1,0:T(8,128)(2,1)S(1)}, bf16[1024,256]{1,0:T(8,128)(2,1)}, u32[]{:S(2)}) copy-start(bf16[1024,256]{1,0:T(8,128)(2,1)} %param.9) | copy-start | bytes 1572868
  135.5 2.0 %copy-start.19 = (f32[256]{0:T(256)S(1)}, f32[256]{0:T(256)}, u32[]{:S(2)}) copy-start(f32[256]{0:T(256)} %param.13) | copy-start | bytes 3076
where the time goes:
time: 142 us; the launch traced here: 141 us
  blocking collectives  45.1 us (32%)
  local copies, waits for them, and re-layouts  40.4 us (28%)
  matrix products  33.5 us (24%)
  other arithmetic  21.5 us (15%)
    dot_general x8, matrix products, product(): return jnp.einsum(pattern, first, second, precision=lax.Precision.HIGH)  28.6 us
    all_gather x1, blocking collectives, shards(): piece = lax.all_gather(own_adjoint[None], 'ctx', axis=0, tiled=True)  25.5 us
    all_gather x1, blocking collectives, shards(): piece = lax.all_gather(own_state[None], 'ctx', axis=0, tiled=True)  19.5 us
    dot_general x1, local copies, waits for them, and re-layouts, shards(): jnp.einsum('tsl,lc->tsc', lag_onehot, tap_values, precision=lax.Precision...  9.14 us
    unnamed x55, local copies, waits for them, and re-layouts  8.71 us
    dot_general x2, local copies, waits for them, and re-layouts, product(): return jnp.einsum(pattern, first, second, precision=lax.Precision.HIGH)  5.63 us
    unnamed x2, other arithmetic  5.42 us
    dot_general x1, matrix products, shards(): jnp.einsum('tsl,lc->tsc', lag_onehot, tap_values, precision=lax.Precision...  4.9 us

commit v1 on v0

--- a/solution.py
+++ b/solution.py
@@ -2,6 +2,28 @@
 import jax.numpy as jnp
 from jax import lax
 from jax.sharding import PartitionSpec as P
+
+
+def joined_along(blocks, dim):
+    lengths = list(blocks.shape[1:])
+    lengths[dim] *= blocks.shape[0]
+    return jnp.moveaxis(blocks, 0, dim).reshape(lengths)
+
+
+def gather_around(value, axis, dim):
+    length = lax.axis_size(axis)
+    pairs = [(i, (i + 1) % length) for i in range(length)]
+    back = [(b, a) for a, b in pairs]
+    lower, upper = ([], [])
+    for step in range(length - 1):
+        if step % 2 == 0:
+            lower.append(lax.ppermute(lower[-1] if lower else value, axis, pairs))
+        else:
+            upper.append(lax.ppermute(upper[-1] if upper else value, axis, back))
+    pieces = jnp.stack([*lower[::-1], value, *upper])
+    shift = lax.axis_index(axis) - len(lower)
+    pieces = pieces[(jnp.arange(length) - shift) % length]
+    return joined_along(pieces, dim)
 
 
 def product(pattern, first, second):
@@ -40,7 +62,7 @@
     within = product("nsc,tsc->ntc", pieces, kernel)
     carried = product("mjkc,jkc->mkc", carry_table, span_states)
     across = product("mkc,tkc->mtc", carried * pole_weight[None], enter_table)
-    piece = lax.all_gather(own_state[None], "ctx", axis=0, tiled=True)
+    piece = gather_around(own_state[None], "ctx", 0)
     anchor = jnp.arange(piece.shape[0])
     distance = position - anchor - 1
     scaled = jnp.exp(

time: 142 us -> 175 us (1.23)
  starting transfers between devices: 0 us -> 28.8 us
  blocking collectives: 45.1 us -> 20.1 us
  local copies, waits for them, and re-layouts: 40.4 us -> 57.8 us
  waiting for transfers between devices: 0 us -> 9.3 us
  matrix products: 33.5 us -> 36.2 us
    ppermute x0 -> x15, starting transfers between devices: none -> 28.8 us  [the longest x7 28.8 us: gather_around(): upper.append(lax.ppermute(upper[-1] if upper else value, axis, back))]
    all_gather x1 -> x0, blocking collectives: 19.5 us -> none  [shards(): piece = lax.all_gather(own_state[None], 'ctx', axis=0, tiled=True)]
    unnamed x55 -> x62, local copies, waits for them, and re-layouts: 8.71 us -> 20.7 us
    ppermute x0 -> x15, waiting for transfers between devices: none -> 9.3 us  [the longest x8 6.17 us: gather_around(): lower.append(lax.ppermute(lower[-1] if lower else value, axis, pairs))]
    gather x0 -> x2, local copies, waits for them, and re-layouts: none -> 5.75 us  [gather_around(): pieces = pieces[(jnp.arange(length) - shift) % length]]
    all_gather x1, blocking collectives: 25.5 us -> 20.1 us  [shards(): piece = lax.all_gather(own_adjoint[None], 'ctx', axis=0, tiled=True)]
    dot_general x8, matrix products: 28.6 us -> 32.4 us  [product(): return jnp.einsum(pattern, first, second, precision=lax.Precision.HIGH)]
    all_gather x1 -> x0, local copies, waits for them, and re-layouts: 3.37 us -> none  [shards(): piece = lax.all_gather(own_state[None], 'ctx', axis=0, tiled=True)]
  transfers between devices with their start and end apart: 0 -> 15, of which waited for: 0 -> 4; matrix products, arithmetic and copies ran while one was open for 0% -> 35% of each run, Pallas kernels for 0% -> 0%
where the time goes in v1:
time: 175 us; the launch traced here: 174 us
  local copies, waits for them, and re-layouts  57.8 us (33%)
  matrix products  36.2 us (21%)
  starting transfers between devices  28.8 us (16%)
  other arithmetic  21.2 us (12%)
  blocking collectives  20.1 us (11%)
  waiting for transfers between devices  9.3 us (5%)
    dot_general x8, matrix products, product(): return jnp.einsum(pattern, first, second, precision=lax.Precision.HIGH)  32.4 us
    ppermute x7, starting transfers between devices, gather_around(): upper.append(lax.ppermute(upper[-1] if upper else value, axis, back))  28.8 us
    unnamed x62, local copies, waits for them, and re-layouts  20.7 us
    all_gather x1, blocking collectives, shards(): piece = lax.all_gather(own_adjoint[None], 'ctx', axis=0, tiled=True)  20.1 us
    dot_general x1, local copies, waits for them, and re-layouts, shards(): jnp.einsum('tsl,lc->tsc', lag_onehot, tap_values, precision=lax.Precision...  9.16 us
    dot_general x2, local copies, waits for them, and re-layouts, product(): return jnp.einsum(pattern, first, second, precision=lax.Precision.HIGH)  6.8 us
    ppermute x8, waiting for transfers between devices, gather_around(): lower.append(lax.ppermute(lower[-1] if lower else value, axis, pairs))  6.17 us
    gather x2, local copies, waits for them, and re-layouts, gather_around(): pieces = pieces[(jnp.arange(length) - shift) % length]  5.75 us
  transfers between devices with their start and end apart: 15, of which 4 were waited for; matrix products, arithmetic and copies ran while one was open for 35% of the time, Pallas kernels for 0%

profile of v1, /device:TPU:0, one launch (start us, length us, event | category | flops | bytes accessed | tf_op | source)
XLA Modules:
  0.0 174.3 jit_solution(6533165474000009464)
XLA Ops:
  5.5 2.5 %copy.113 = f32[16,64,256]{1,0,2:T(8,128)S(1)} copy(f32[16,64,256]{2,1,0:T(8,128)} %bitcast.122) | data formatting | bytes 2097152 | tf_op jit(solution)/shard_map/reshape | solution.py:81
  8.0 4.1 %multiply_exponential_fusion = (f32[16,16,256]{1,0,2:T(8,128)}, f32[16,256]{0,1:T(8,128)S(1)}, f32[256,16,16]{1,2,0:T(8,128)}) fusion(f32[16]{0:T(128)S(1)} %iota_multiply_fusion, f32[16,256]{0,1:T(8,128)S(1)} %copy.88, f32[16,64,256]{1,0,2:T(8,128)S(1)} %copy.113, f32[64]{0:T(128)S(1)} %iota_add_fusion), kind=kOutput, calls=%fused_computation.21 | convolution fusion | flops 25620480 | bytes 1605952 | tf_op jit(solution)/shard_map/ntc,tkc->nkc/dot_general | solution.py:30
  12.1 2.4 %rev.3 = f32[16,16,256]{1,0,2:T(8,128)S(1)} reverse(f32[16,16,256]{1,0,2:T(8,128)} %get-tuple-element.12), dimensions={0} | reverse | bytes 524288 | tf_op jit(solution)/shard_map/rev | solution.py:47
  14.5 3.7 %fusion.5 = (f32[16,256]{0,1:T(8,128)S(1)}, f32[256,16,16]{1,2,0:T(8,128)}) fusion(f32[16,16,256]{1,0,2:T(8,128)S(1)} %rev.3, bf16[16,64,256]{1,0,2:T(8,128)(2,1)S(1)} %copy.91, f32[64]{0:T(128)} %iota_subtract_fusion.1, f32[16,256]{0,1:T(8,128)S(1)} %copy.88), kind=kOutput, calls=%fused_computation.11 | convolution fusion | flops 25554944 | bytes 1081600 | tf_op jit(solution)/shard_map/nsc,skc->nkc/dot_general | solution.py:30
  18.8 5.4 %collective-permute-start.8 = (f32[1,16,256]{2,1,0:T(8,128)}, f32[1,16,256]{2,1,0:T(8,128)}, u32[]{:S(2)}, u32[]{:S(2)}) collective-permute-start(f32[1,16,256]{2,1,0:T(8,128)} %bitcast.11), channel_id=1, source_target_pairs={{1,0},{2,1},{3,2},{4,3},{5,4},{6,5},{7,6},{8,7},{9,8},{10,9},{11,1... | collective-permute-start | bytes 49160 | tf_op jit(solution)/shard_map/ppermute | solution.py:22
  26.3 3.2 %copy.137 = f32[16,256,16]{1,0,2:T(8,128)} copy(f32[16,256,16]{0,2,1:T(8,128)} %bitcast.119) | data formatting | bytes 524288
  29.5 2.7 %multiply_reduce_fusion = f32[16,256,16]{1,0,2:T(8,128)} fusion(f32[16,256,16]{1,0,2:T(8,128)} %copy.137, f32[16,16]{1,0:T(8,128)} %convert_multiply_fusion.6, f32[16,256]{1,0:T(8,128)S(1)} %negate_bitcast_fusion, pred[16,16]{1,0:T(8,128)(4,1)} %iota_compare_fusion.2), kind=kLoop, calls=%fused_computation.1 | loop fusion | flops 4128768 | bytes 541952
  32.1 3.4 %copy.134 = f32[16,256,16]{0,2,1:T(8,128)} copy(f32[16,256,16]{1,0,2:T(8,128)} %multiply_reduce_fusion) | data formatting | bytes 524288 | tf_op jit(solution)/shard_map/mjkc,mkc->jkc/dot_general | solution.py:30
  35.5 3.2 %copy.136 = f32[16,256,16]{1,0,2:T(8,128)} copy(f32[16,256,16]{0,2,1:T(8,128)} %bitcast.120) | data formatting | bytes 524288
  38.7 2.8 %multiply_reduce_fusion.1 = f32[16,256,16]{1,0,2:T(8,128)} fusion(f32[16,256,16]{1,0,2:T(8,128)} %copy.136, f32[16,16]{1,0:T(8,128)} %convert_multiply_fusion.6, f32[16,256]{1,0:T(8,128)S(1)} %negate_bitcast_fusion, pred[16,16]{1,0:T(8,128)(4,1)} %iota_compare_fusion.2), kind=kLoop, calls=%fused_computation.2 | loop fusion | flops 4128768 | bytes 541952
  41.5 3.4 %copy.126 = f32[16,256,16]{0,2,1:T(8,128)} copy(f32[16,256,16]{1,0,2:T(8,128)} %multiply_reduce_fusion.1) | data formatting | bytes 524288 | tf_op jit(solution)/shard_map/mjkc,jkc->mkc/dot_general | solution.py:30
  44.9 4.4 %fusion = f32[256,64,16]{1,2,0:T(8,128)} fusion(f32[16,256,16]{0,2,1:T(8,128)} %copy.134, f32[16,256]{0,1:T(8,128)S(1)} %bitcast.123, f32[64]{0:T(128)S(1)} %copy-done.10, f32[16,256]{0,1:T(8,128)S(1)} %copy.88), kind=kOutput, calls=%fused_computation.4 | convolution fusion | flops 25493504 | bytes 1343744 | tf_op jit(solution)/shard_map/jkc,skc->jsc/dot_general | solution.py:30
  49.3 2.5 %fusion.3 = f32[256,64,16]{1,2,0:T(8,128)} fusion(f32[16,256,16]{0,2,1:T(8,128)S(1)} %copy-done.3, f32[16,256]{0,1:T(8,128)S(1)} %bitcast.124, f32[64]{0:T(128)S(1)} %copy-done.13, f32[16,256]{0,1:T(8,128)S(1)} %copy.88), kind=kOutput, calls=%fused_computation.8 | convolution fusion | flops 25493504 | bytes 1343744 | tf_op jit(solution)/shard_map/mkc,tkc->mtc/dot_general | solution.py:30
  53.5 6.2 %collective-permute-done.1 = f32[1,16,256]{2,1,0:T(8,128)} collective-permute-done((f32[1,16,256]{2,1,0:T(8,128)}, f32[1,16,256]{2,1,0:T(8,128)}, u32[]{:S(2)}, u32[]{:S(2)}) %collective-permute-start.1) | collective-permute-done | bytes 16416 | tf_op jit(solution)/shard_map/ppermute | solution.py:20
  59.7 3.8 %fusion.14 = f32[64,64,256]{2,1,0:T(8,128)} fusion(s32[64,64]{1,0:T(8,128)S(1)} %iota_subtract_fusion, f32[64,256]{0,1:T(8,128)S(1)} %multiply_reduce_fusion.4), kind=kOutput, calls=%fused_computation.29 | convolution fusion | flops 805568512 | bytes 4276224 | tf_op jit(solution)/shard_map/tsl,lc->tsc/dot_general | solution.py:58
  63.5 4.5 %collective-permute-start.9 = (f32[1,16,256]{2,1,0:T(8,128)}, f32[1,16,256]{2,1,0:T(8,128)S(1)}, u32[]{:S(2)}, u32[]{:S(2)}) collective-permute-start(f32[1,16,256]{2,1,0:T(8,128)} %collective-permute-done.8), channel_id=1, source_target_pairs={{1,0},{2,1},{3,2},{4,3},{5,4},{6,5},{7,6},{8,7},{9,8},{10,9},{11,1... | collective-permute-start | bytes 49160 | tf_op jit(solution)/shard_map/ppermute | solution.py:22
  68.0 20.1 %all-gather = f32[256,256]{1,0:T(8,128)} all-gather(f32[16,256]{1,0:T(8,128)S(1)} %copy.115), channel_id=2, replica_groups=mesh['groups'=2,'ctx'=16] {'ctx'}, dimensions={0}, use_global_device_ids=true | all-gather | bytes 278528 | tf_op jit(solution)/shard_map/all_gather | solution.py:87
  90.7 4.4 %collective-permute-start.11 = (f32[1,16,256]{2,1,0:T(8,128)S(1)}, f32[1,16,256]{2,1,0:T(8,128)S(1)}, u32[]{:S(2)}, u32[]{:S(2)}) collective-permute-start(f32[1,16,256]{2,1,0:T(8,128)S(1)} %collective-permute-done.10), channel_id=1, source_target_pairs={{1,0},{2,1},{3,2},{4,3},{5,4},{6,5},{7,6},{8,7},{9,8},{10,9},{11,1... | collective-permute-start | bytes 49160 | tf_op jit(solution)/shard_map/ppermute | solution.py:22
  96.6 4.4 %collective-permute-start.12 = (f32[1,16,256]{2,1,0:T(8,128)S(1)}, f32[1,16,256]{2,1,0:T(8,128)S(1)}, u32[]{:S(2)}, u32[]{:S(2)}) collective-permute-start(f32[1,16,256]{2,1,0:T(8,128)S(1)} %collective-permute-done.11), channel_id=1, source_target_pairs={{1,0},{2,1},{3,2},{4,3},{5,4},{6,5},{7,6},{8,7},{9,8},{10,9},{11,1... | collective-permute-start | bytes 49160 | tf_op jit(solution)/shard_map/ppermute | solution.py:22
  102.5 4.4 %collective-permute-start.13 = (f32[1,16,256]{2,1,0:T(8,128)S(1)}, f32[1,16,256]{2,1,0:T(8,128)S(1)}, u32[]{:S(2)}, u32[]{:S(2)}) collective-permute-start(f32[1,16,256]{2,1,0:T(8,128)S(1)} %collective-permute-done.12), channel_id=1, source_target_pairs={{1,0},{2,1},{3,2},{4,3},{5,4},{6,5},{7,6},{8,7},{9,8},{10,9},{11,1... | collective-permute-start | bytes 49160 | tf_op jit(solution)/shard_map/ppermute | solution.py:22
  107.5 9.2 %copy.90 = f32[64,64,256]{1,0,2:T(8,128)} copy(f32[64,64,256]{2,1,0:T(8,128)} %fusion.14) | data formatting | bytes 8388608 | tf_op jit(solution)/shard_map/tsl,lc->tsc/dot_general | solution.py:58
  116.6 3.5 %copy.116 = f32[16,16,256]{1,0,2:T(8,128)} copy(f32[16,16,256]{2,1,0:T(8,128)} %bitcast.126) | data formatting | bytes 524288 | tf_op jit(solution)/shard_map/all_gather | solution.py:87
  120.1 4.4 %collective-permute-start.14 = (f32[1,16,256]{2,1,0:T(8,128)S(1)}, f32[1,16,256]{2,1,0:T(8,128)S(1)}, u32[]{:S(2)}, u32[]{:S(2)}) collective-permute-start(f32[1,16,256]{2,1,0:T(8,128)S(1)} %collective-permute-done.13), channel_id=1, source_target_pairs={{1,0},{2,1},{3,2},{4,3},{5,4},{6,5},{7,6},{8,7},{9,8},{10,9},{11,1... | collective-permute-start | bytes 49160 | tf_op jit(solution)/shard_map/ppermute | solution.py:22
  138.6 2.3 %gather_fusion = f32[16,16,256]{2,1,0:T(8,128)} fusion(f32[16,16,256]{2,1,0:T(8,128)} %bitcast.42, s32[1024]{0:T(1024)} %pad_clamp_fusion), kind=kCustom, calls=%fused_computation | custom fusion | bytes 524352 | tf_op jit(solution)/shard_map/gather | solution.py:25
  140.9 3.4 %copy.110 = f32[16,16,256]{1,0,2:T(8,128)} copy(f32[16,16,256]{2,1,0:T(8,128)} %gather_fusion) | data formatting | bytes 524288 | tf_op jit(solution)/shard_map/gather | solution.py:25
  144.3 4.0 %multiply_reduce_fusion.2 = (f32[16,256]{0,1:T(8,128)S(1)}, f32[16,256]{0,1:T(8,128)S(1)}) fusion(f32[16,16,256]{1,0,2:T(8,128)} %copy.116, f32[16]{0:T(128)S(1)} %copy-done.18, f32[16,256]{0,1:T(8,128)S(1)} %copy.88, pred[16]{0:T(512)(128)(4,1)S(1)} %copy-done.21, f32[16,16,256]{1,0,2:T(8,128)} %copy.110, f32[16]{0:T(128)S(1)} %copy-done.19, ...), kind=kLoop, calls=%fused_computation.15 | loop fusion | flops 516096 | bytes 573600 | tf_op jit(solution)/shard_map/reduce_sum | solution.py:95
  149.8 5.4 %add_bitcast_fusion = f32[16,64,256]{1,0,2:T(8,128)S(1)} fusion(f32[256,64,16]{1,2,0:T(8,128)S(1)} %fusion.6, f32[256,64,16]{1,2,0:T(8,128)} %fusion, f32[64,64,256]{1,0,2:T(8,128)S(1)} %copy-done, f32[16,64,256]{1,0,2:T(8,128)} %copy-done.1), kind=kOutput, calls=%fused_computation.12 | convolution fusion | flops 101187584 | bytes 8388608 | tf_op jit(solution)/shard_map/ntc,tsc->nsc/dot_general | solution.py:30
  155.3 2.0 %copy.117 = f32[16,64,256]{2,1,0:T(8,128)} copy(f32[16,64,256]{1,0,2:T(8,128)S(1)} %add_bitcast_fusion) | data formatting | bytes 2097152 | tf_op jit(solution)/shard_map/add | solution.py:97
  157.3 1.6 fusion.9
  158.9 9.3 %add_bitcast_fusion.1 = f32[16,64,256]{1,0,2:T(8,128)} fusion(f32[256,64,16]{1,2,0:T(8,128)S(1)} %fusion.9, f32[256,64,16]{1,2,0:T(8,128)S(1)} %copy-done.2, f32[64,64,256]{1,0,2:T(8,128)} %copy.90, bf16[16,64,256]{1,0,2:T(8,128)(2,1)S(1)} %copy.91), kind=kOutput, calls=%fused_computation.17 | convolution fusion | flops 101187584 | bytes 7864320 | tf_op jit(solution)/shard_map/nsc,tsc->ntc/dot_general | solution.py:30
  168.2 2.7 %copy.111 = f32[16,64,256]{2,1,0:T(8,128)S(1)} copy(f32[16,64,256]{1,0,2:T(8,128)} %add_bitcast_fusion.1) | data formatting | bytes 2097152 | tf_op jit(solution)/shard_map/add | solution.py:75
  170.9 3.4 %fusion.19 = (bf16[1024,256]{1,0:T(8,128)(2,1)}, bf16[1024,256]{1,0:T(8,128)(2,1)}, bf16[1024,256]{1,0:T(8,128)(2,1)}, bf16[1024,256]{1,0:T(8,128)(2,1)}) fusion(bf16[1024,256]{1,0:T(8,128)(2,1)} %param.10, f32[16,64,256]{2,1,0:T(8,128)S(1)} %copy.111, bf16[1024,256]{1,0:T(8,128)(2,1)S(1)} %copy-done.5, f32[256]{0:T(256)S(1)} %copy-done.15, ...), kind=kLoop, calls=%fused_computation.40 | loop fusion | flops 4718592 | bytes 6816768 | tf_op jit(solution)/shard_map/convert_element_type | solution.py:79
  (104 shorter events, 30.8 us)
Async XLA Ops:
  0.6 3.7 %copy-start.8 = (bf16[1024,256]{1,0:T(8,128)(2,1)S(1)}, bf16[1024,256]{1,0:T(8,128)(2,1)}, u32[]{:S(2)}) copy-start(bf16[1024,256]{1,0:T(8,128)(2,1)} %param.10) | copy-start | bytes 1572868
  0.6 3.7 %copy-start.9 = (bf16[1024,256]{1,0:T(8,128)(2,1)S(1)}, bf16[1024,256]{1,0:T(8,128)(2,1)}, u32[]{:S(2)}) copy-start(bf16[1024,256]{1,0:T(8,128)(2,1)} %param.7) | copy-start | bytes 1572868
  0.7 7.3 %copy-start.12 = (f32[64]{0:T(128)}, f32[64]{0:T(128)S(1)}, u32[]{:S(2)}) copy-start(f32[64]{0:T(128)S(1)} %iota_add_fusion) | copy-start | bytes 772
  1.2 6.8 %copy-start.16 = (f32[16]{0:T(128)}, f32[16]{0:T(128)S(1)}, u32[]{:S(2)}) copy-start(f32[16]{0:T(128)S(1)} %iota_multiply_fusion) | copy-start | bytes 196
  8.0 4.1 %copy-start.1 = (f32[16,64,256]{1,0,2:T(8,128)}, f32[16,64,256]{1,0,2:T(8,128)S(1)}, u32[]{:S(2)}) copy-start(f32[16,64,256]{1,0,2:T(8,128)S(1)} %copy.113) | copy-start | bytes 3145732
  18.8 44.7 %collective-permute-start.8 = (f32[1,16,256]{2,1,0:T(8,128)}, f32[1,16,256]{2,1,0:T(8,128)}, u32[]{:S(2)}, u32[]{:S(2)}) collective-permute-start(f32[1,16,256]{2,1,0:T(8,128)} %bitcast.11), channel_id=1, source_target_pairs={{1,0},{2,1},{3,2},{4,3},{5,4},{6,5},{7,6},{8,7},{9,8},{10,9},{11,1... | collective-permute-start | bytes 49160 | tf_op jit(solution)/shard_map/ppermute | solution.py:22
  24.3 29.2 %collective-permute-start = (f32[1,16,256]{2,1,0:T(8,128)}, f32[1,16,256]{2,1,0:T(8,128)}, u32[]{:S(2)}, u32[]{:S(2)}) collective-permute-start(f32[1,16,256]{2,1,0:T(8,128)} %bitcast.11), channel_id=1, source_target_pairs={{0,1},{1,2},{2,3},{3,4},{4,5},{5,6},{6,7},{7,8},{8,9},{9,10},{10,1... | collective-permute-start | bytes 49160 | tf_op jit(solution)/shard_map/ppermute | solution.py:20
  41.5 3.4 %copy-start.10 = (f32[64]{0:T(128)S(1)}, f32[64]{0:T(128)}, u32[]{:S(2)}) copy-start(f32[64]{0:T(128)} %iota_subtract_fusion.1) | copy-start | bytes 772
  44.9 4.4 %copy-start.3 = (f32[16,256,16]{0,2,1:T(8,128)S(1)}, f32[16,256,16]{0,2,1:T(8,128)}, u32[]{:S(2)}) copy-start(f32[16,256,16]{0,2,1:T(8,128)} %copy.126) | copy-start | bytes 786436
  44.9 4.4 %copy-start.13 = (f32[64]{0:T(128)S(1)}, f32[64]{0:T(128)}, u32[]{:S(2)}) copy-start(f32[64]{0:T(128)} %copy-done.12) | copy-start | bytes 772
  53.4 6.2 %collective-permute-start.1 = (f32[1,16,256]{2,1,0:T(8,128)}, f32[1,16,256]{2,1,0:T(8,128)}, u32[]{:S(2)}, u32[]{:S(2)}) collective-permute-start(f32[1,16,256]{2,1,0:T(8,128)} %collective-permute-done), channel_id=1, source_target_pairs={{0,1},{1,2},{2,3},{3,4},{4,5},{5,6},{6,7},{7,8},{8,9},{9,10},{10,1... | collective-permute-start | bytes 49160 | tf_op jit(solution)/shard_map/ppermute | solution.py:20
  59.7 8.3 %collective-permute-start.2 = (f32[1,16,256]{2,1,0:T(8,128)}, f32[1,16,256]{2,1,0:T(8,128)}, u32[]{:S(2)}, u32[]{:S(2)}) collective-permute-start(f32[1,16,256]{2,1,0:T(8,128)} %collective-permute-done.1), channel_id=1, source_target_pairs={{0,1},{1,2},{2,3},{3,4},{4,5},{5,6},{6,7},{7,8},{8,9},{9,10},{10,1... | collective-permute-start | bytes 49160 | tf_op jit(solution)/shard_map/ppermute | solution.py:20
  63.5 24.6 %collective-permute-start.9 = (f32[1,16,256]{2,1,0:T(8,128)}, f32[1,16,256]{2,1,0:T(8,128)S(1)}, u32[]{:S(2)}, u32[]{:S(2)}) collective-permute-start(f32[1,16,256]{2,1,0:T(8,128)} %collective-permute-done.8), channel_id=1, source_target_pairs={{1,0},{2,1},{3,2},{4,3},{5,4},{6,5},{7,6},{8,7},{9,8},{10,9},{11,1... | collective-permute-start | bytes 49160 | tf_op jit(solution)/shard_map/ppermute | solution.py:22
  68.0 21.3 %collective-permute-start.3 = (f32[1,16,256]{2,1,0:T(8,128)}, f32[1,16,256]{2,1,0:T(8,128)S(1)}, u32[]{:S(2)}, u32[]{:S(2)}) collective-permute-start(f32[1,16,256]{2,1,0:T(8,128)} %collective-permute-done.2), channel_id=1, source_target_pairs={{0,1},{1,2},{2,3},{3,4},{4,5},{5,6},{6,7},{7,8},{8,9},{9,10},{10,1... | collective-permute-start | bytes 49160 | tf_op jit(solution)/shard_map/ppermute | solution.py:20
  88.1 2.6 %collective-permute-start.10 = (f32[1,16,256]{2,1,0:T(8,128)S(1)}, f32[1,16,256]{2,1,0:T(8,128)S(1)}, u32[]{:S(2)}, u32[]{:S(2)}) collective-permute-start(f32[1,16,256]{2,1,0:T(8,128)S(1)} %collective-permute-done.9), channel_id=1, source_target_pairs={{1,0},{2,1},{3,2},{4,3},{5,4},{6,5},{7,6},{8,7},{9,8},{10,9},{11,1... | collective-permute-start | bytes 49160 | tf_op jit(solution)/shard_map/ppermute | solution.py:22
  89.3 5.9 %collective-permute-start.4 = (f32[1,16,256]{2,1,0:T(8,128)S(1)}, f32[1,16,256]{2,1,0:T(8,128)S(1)}, u32[]{:S(2)}, u32[]{:S(2)}) collective-permute-start(f32[1,16,256]{2,1,0:T(8,128)S(1)} %collective-permute-done.3), channel_id=1, source_target_pairs={{0,1},{1,2},{2,3},{3,4},{4,5},{5,6},{6,7},{7,8},{8,9},{9,10},{10,1... | collective-permute-start | bytes 49160 | tf_op jit(solution)/shard_map/ppermute | solution.py:20
  90.7 5.9 %collective-permute-start.11 = (f32[1,16,256]{2,1,0:T(8,128)S(1)}, f32[1,16,256]{2,1,0:T(8,128)S(1)}, u32[]{:S(2)}, u32[]{:S(2)}) collective-permute-start(f32[1,16,256]{2,1,0:T(8,128)S(1)} %collective-permute-done.10), channel_id=1, source_target_pairs={{1,0},{2,1},{3,2},{4,3},{5,4},{6,5},{7,6},{8,7},{9,8},{10,9},{11,1... | collective-permute-start | bytes 49160 | tf_op jit(solution)/shard_map/ppermute | solution.py:22
  95.2 5.9 %collective-permute-start.5 = (f32[1,16,256]{2,1,0:T(8,128)S(1)}, f32[1,16,256]{2,1,0:T(8,128)S(1)}, u32[]{:S(2)}, u32[]{:S(2)}) collective-permute-start(f32[1,16,256]{2,1,0:T(8,128)S(1)} %collective-permute-done.4), channel_id=1, source_target_pairs={{0,1},{1,2},{2,3},{3,4},{4,5},{5,6},{6,7},{7,8},{8,9},{9,10},{10,1... | collective-permute-start | bytes 49160 | tf_op jit(solution)/shard_map/ppermute | solution.py:20
  96.6 5.9 %collective-permute-start.12 = (f32[1,16,256]{2,1,0:T(8,128)S(1)}, f32[1,16,256]{2,1,0:T(8,128)S(1)}, u32[]{:S(2)}, u32[]{:S(2)}) collective-permute-start(f32[1,16,256]{2,1,0:T(8,128)S(1)} %collective-permute-done.11), channel_id=1, source_target_pairs={{1,0},{2,1},{3,2},{4,3},{5,4},{6,5},{7,6},{8,7},{9,8},{10,9},{11,1... | collective-permute-start | bytes 49160 | tf_op jit(solution)/shard_map/ppermute | solution.py:22
  101.0 5.9 %collective-permute-start.6 = (f32[1,16,256]{2,1,0:T(8,128)S(1)}, f32[1,16,256]{2,1,0:T(8,128)S(1)}, u32[]{:S(2)}, u32[]{:S(2)}) collective-permute-start(f32[1,16,256]{2,1,0:T(8,128)S(1)} %collective-permute-done.5), channel_id=1, source_target_pairs={{0,1},{1,2},{2,3},{3,4},{4,5},{5,6},{6,7},{7,8},{8,9},{9,10},{10,1... | collective-permute-start | bytes 49160 | tf_op jit(solution)/shard_map/ppermute | solution.py:20
  102.5 17.6 %collective-permute-start.13 = (f32[1,16,256]{2,1,0:T(8,128)S(1)}, f32[1,16,256]{2,1,0:T(8,128)S(1)}, u32[]{:S(2)}, u32[]{:S(2)}) collective-permute-start(f32[1,16,256]{2,1,0:T(8,128)S(1)} %collective-permute-done.12), channel_id=1, source_target_pairs={{1,0},{2,1},{3,2},{4,3},{5,4},{6,5},{7,6},{8,7},{9,8},{10,9},{11,1... | collective-permute-start | bytes 49160 | tf_op jit(solution)/shard_map/ppermute | solution.py:22
  106.9 17.7 %collective-permute-start.7 = (f32[1,16,256]{2,1,0:T(8,128)S(1)}, f32[1,16,256]{2,1,0:T(8,128)}, u32[]{:S(2)}, u32[]{:S(2)}) collective-permute-start(f32[1,16,256]{2,1,0:T(8,128)S(1)} %collective-permute-done.6), channel_id=1, source_target_pairs={{0,1},{1,2},{2,3},{3,4},{4,5},{5,6},{6,7},{7,8},{8,9},{9,10},{10,1... | collective-permute-start | bytes 49160 | tf_op jit(solution)/shard_map/ppermute | solution.py:20
  120.1 17.9 %collective-permute-start.14 = (f32[1,16,256]{2,1,0:T(8,128)S(1)}, f32[1,16,256]{2,1,0:T(8,128)S(1)}, u32[]{:S(2)}, u32[]{:S(2)}) collective-permute-start(f32[1,16,256]{2,1,0:T(8,128)S(1)} %collective-permute-done.13), channel_id=1, source_target_pairs={{1,0},{2,1},{3,2},{4,3},{5,4},{6,5},{7,6},{8,7},{9,8},{10,9},{11,1... | collective-permute-start | bytes 49160 | tf_op jit(solution)/shard_map/ppermute | solution.py:22
  126.5 17.8 %copy-start.18 = (f32[16]{0:T(128)S(1)}, f32[16]{0:T(128)}, u32[]{:S(2)}) copy-start(f32[16]{0:T(128)} %get-tuple-element.19) | copy-start | bytes 196
  126.5 17.8 %copy-start.19 = (f32[16]{0:T(128)S(1)}, f32[16]{0:T(128)}, u32[]{:S(2)}) copy-start(f32[16]{0:T(128)} %get-tuple-element.20) | copy-start | bytes 196
  126.5 17.8 %copy-start.20 = (pred[16]{0:T(512)(128)(4,1)S(1)}, pred[16]{0:T(512)(128)(4,1)}, u32[]{:S(2)}) copy-start(pred[16]{0:T(512)(128)(4,1)} %get-tuple-element.21) | copy-start | bytes 52
  127.1 17.2 %copy-start.21 = (pred[16]{0:T(512)(128)(4,1)S(1)}, pred[16]{0:T(512)(128)(4,1)}, u32[]{:S(2)}) copy-start(pred[16]{0:T(512)(128)(4,1)} %get-tuple-element.22) | copy-start | bytes 52
  140.9 7.5 %copy-start.11 = (f32[64]{0:T(128)S(1)}, f32[64]{0:T(128)}, u32[]{:S(2)}) copy-start(f32[64]{0:T(128)} %iota_subtract_fusion.1) | copy-start | bytes 772
  144.3 5.5 %copy-start = (f32[64,64,256]{1,0,2:T(8,128)S(1)}, f32[64,64,256]{1,0,2:T(8,128)}, u32[]{:S(2)}) copy-start(f32[64,64,256]{1,0,2:T(8,128)} %copy.90) | copy-start | bytes 12582916
  168.2 2.7 %copy-start.6 = (f32[16,64,256]{2,1,0:T(8,128)S(1)}, f32[16,64,256]{2,1,0:T(8,128)}, u32[]{:S(2)}) copy-start(f32[16,64,256]{2,1,0:T(8,128)} %copy.117) | copy-start | bytes 3145732
  168.2 2.7 %copy-start.7 = (bf16[1024,256]{1,0:T(8,128)(2,1)S(1)}, bf16[1024,256]{1,0:T(8,128)(2,1)}, u32[]{:S(2)}) copy-start(bf16[1024,256]{1,0:T(8,128)(2,1)} %param.9) | copy-start | bytes 1572868
  168.2 2.7 %copy-start.15 = (f32[256]{0:T(256)S(1)}, f32[256]{0:T(256)}, u32[]{:S(2)}) copy-start(f32[256]{0:T(256)} %param.13) | copy-start | bytes 3076
  (5 other events, 10.5 us)
